TPU v7x, 512 devices: a whole 4x4x16 slice. The times are simulated.
512 devices in a mesh: seq: 64 (over x, z), tp: 8 (over y, core).
Axes of the slice: x: 4, y: 4, z: 16, core: 2. Of those that a mesh axis runs over, the one named last changes fastest.
Arguments:
- queries: bfloat16 [16384, 4096], P('seq', 'tp'), may hold values from -122 to 122
- suffix_k: bfloat16 [16384, 1024], P('seq', 'tp'), may hold values from -6 to 6
- suffix_v: bfloat16 [16384, 1024], P('seq', 'tp'), may hold values from -6 to 6
- prefix_k: bfloat16 [8192, 1024], P('seq', 'tp'), may hold values from -8 to 8
- prefix_v: bfloat16 [8192, 1024], P('seq', 'tp'), may hold values from -6 to 6
- prefix_block: int32 [64], P('seq'), may hold values from 0 to 63, each once
- request_ids: int32 [64, 256], P('seq'), may hold values from 0 to 7, never falling along the last dimension, each value on 1 to 64 neighbouring positions
- out_weight: bfloat16 [4096, 4096], P('tp', 'seq'), may hold values from -0.09375 to 0.09375
Outputs:
- mixed: bfloat16 [16384, 4096], P('seq', 'tp')
Inputs may be any that keep to these rules, and one draw needn't show every extreme that they name: `request_ids`: each row packs 8 requests in order, each of 1 to 64 slots, one of exactly 64. `prefix_block`: each prefix block appears once.
All inputs are finite; a program needn't handle non-finite values.
Results may differ from a plain program's by a relative error of at most 0.019.
Values may be sent and summed in bfloat16 or wider, within the bound.
A program may use at most 128 MiB of HBM per device.

v0:
```python
import math

import jax
import jax.numpy as jnp
from jax import lax
from jax.sharding import PartitionSpec as P

HD = 128
SINKS = 4


def update(carry, grouped, keys, values, allowed):
    run_max, run_sum, totals = carry
    key_rows = keys.shape[0]
    kv_heads = grouped.shape[1]
    key_heads = keys.reshape(key_rows, kv_heads, HD)
    value_heads = values.reshape(key_rows, kv_heads, HD)
    scores = jnp.einsum(
        "shgd,nhd->hgsn", grouped, key_heads, preferred_element_type=jnp.float32
    ) * (1.0 / math.sqrt(HD))
    scores = jnp.where(allowed, scores, jnp.float32(-1e30))
    new_max = jnp.maximum(run_max, jnp.max(scores, axis=-1))
    weights = jnp.where(allowed, jnp.exp(scores - new_max[..., None]), jnp.float32(0.0))
    factor = jnp.exp(run_max - new_max)
    run_sum = run_sum * factor + jnp.sum(weights, axis=-1)
    added = jnp.einsum(
        "hgsn,nhd->hgsd",
        weights.astype(jnp.bfloat16),
        value_heads,
        preferred_element_type=jnp.float32,
    )
    totals = totals * factor[..., None] + added
    return (new_max, run_sum, totals)


def local(queries, suffix_k, suffix_v, prefix_k, prefix_v, prefix_block, request_ids, out_weight):
    tokens_here = queries.shape[0]
    kv_heads = suffix_k.shape[1] // HD
    group_size = queries.shape[1] // (kv_heads * HD)
    block_rows = prefix_k.shape[0]
    prefix_len = block_rows * lax.axis_size("seq")
    window = prefix_len // 2
    request = request_ids[0]
    slots = jnp.arange(tokens_here, dtype=jnp.int32)
    same = request[:, None] == request[None, :]
    offsets = jnp.sum((same & (slots[None, :] < slots[:, None])).astype(jnp.int32), axis=1)
    query_pos = prefix_len + offsets
    own_mask = same & (slots[None, :] <= slots[:, None])
    grouped = queries.reshape(tokens_here, kv_heads, group_size, HD)
    prefix_pos = prefix_block[0] * block_rows + jnp.arange(block_rows, dtype=jnp.int32)
    empty = (
        jnp.full((kv_heads, group_size, tokens_here), -1e30, jnp.float32),
        jnp.zeros((kv_heads, group_size, tokens_here), jnp.float32),
        jnp.zeros((kv_heads, group_size, tokens_here, HD), jnp.float32),
    )
    keys = lax.all_gather(prefix_k, "seq", axis=0, tiled=True)
    values = lax.all_gather(prefix_v, "seq", axis=0, tiled=True)
    positions = lax.all_gather(prefix_pos, "seq", axis=0, tiled=True)
    allowed = (positions[None, :] >= query_pos[:, None] - window + 1) | (positions[None, :] < SINKS)
    carry = update(empty, grouped, keys, values, allowed)
    carry = update(carry, grouped, suffix_k, suffix_v, own_mask)
    run_max, run_sum, totals = carry
    attended = (
        (totals / run_sum[..., None])
        .transpose(2, 0, 1, 3)
        .reshape(tokens_here, kv_heads * group_size * HD)
        .astype(jnp.bfloat16)
    )
    whole_weight = lax.all_gather(out_weight, "seq", axis=1, tiled=True)
    partial_out = jnp.dot(attended, whole_weight, preferred_element_type=jnp.float32)
    return lax.psum_scatter(partial_out.astype(jnp.bfloat16), "tp", scatter_dimension=1, tiled=True)


def solution(mesh):
    placed = (
        P("seq", "tp"),
        P("seq", "tp"),
        P("seq", "tp"),
        P("seq", "tp"),
        P("seq", "tp"),
        P("seq"),
        P("seq", None),
        P("tp", "seq"),
    )
    return jax.shard_map(
        local, mesh=mesh, in_specs=placed, out_specs=P("seq", "tp"), check_vma=False
    )
```

profile of v0, /device:TPU:6, one launch (start us, length us, event | category | flops | bytes accessed | tf_op | source)
XLA Modules:
  0.0 482.6 jit_solution(17411898486618395844)
XLA Ops:
  6.5 0.0 copy-start
  6.5 0.0 all-gather.5.cloned.1.call-start
  6.5 0.7 all-gather.5.cloned.1.call-update
  7.3 0.0 all-gather.7.cloned.1.call-start
  7.3 1.5 copy.16
  8.8 0.0 all-gather.7.cloned.1.call-update
  8.8 0.0 all-gather.9.cloned.1.call-start
  8.9 0.7 all-gather.9.cloned.1.call-update
  9.5 0.0 reduce-scatter.2.cloned.1.call-start
  10.2 78.8 %all-gather = s32[64,1,128]{2,1,0:T(1,128)S(1)} all-gather(s32[1,1,128]{2,1,0:T(1,128)S(1)} %add_bitcast_fusion), channel_id=1, replica_groups=mesh['seq'=64,'tp'=8] {'seq'}, dimensions={0}, use_global_device_ids=true | all-gather | bytes 33280 | tf_op jit(solution)/shard_map/all_gather | solution.py:58
  89.1 0.9 convert_reduce_fusion
  89.9 6.1 %compare_or_fusion = pred[256,8192]{0,1:T(8,128)(4,1)S(1)} fusion(s32[256]{0:T(256)S(1)} %broadcast_add_fusion, s32[8192]{0:T(1024)S(1)} %bitcast.84, pred[8192]{0:T(1024)(128)(4,1)S(1)} %broadcast_compare_fusion), kind=kLoop, calls=%fused_computation.8 | loop fusion | flops 4194304 | bytes 2139136 | tf_op jit(solution)/shard_map/or | solution.py:59
  96.1 0.9 compare_and_fusion
  96.9 0.0 copy-done
  96.9 1.2 fusion.42
  98.1 56.4 %all-gather.5.cloned.1.call-done = bf16[8192,128]{1,0:T(8,128)(2,1)} async-done(((bf16[128,128]{1,0:T(8,128)(2,1)}), bf16[8192,128]{1,0:T(8,128)(2,1)}) %all-gather.5.cloned.1.call-update) | async-done | bytes 2097168 | tf_op jit(solution)/shard_map/all_gather | solution.py:56
  154.5 14.9 %fusion = (f32[4,256]{1,0:T(4,128)S(1)}, f32[8192,256,4]{1,0,2:T(8,128)}) fusion(pred[256,8192]{0,1:T(8,128)(4,1)S(1)} %compare_or_fusion, bf16[8192,128]{1,0:T(8,128)(2,1)} %all-gather.5.cloned.1.call-done, bf16[256,512]{1,0:T(8,128)(2,1)S(1)} %copy-done), kind=kOutput, calls=%fused_computation.2 | convolution fusion | flops 2172648448 | bytes 38014976 | tf_op jit(solution)/shard_map/shgd,nhd->hgsn/dot_general | solution.py:18
  169.4 0.2 fusion.24
  169.6 15.0 %fusion.1 = f32[4,256]{1,0:T(4,128)S(1)} fusion(f32[8192,256,4]{1,0,2:T(8,128)} %get-tuple-element.11, f32[4,256]{1,0:T(4,128)S(1)} %get-tuple-element.9, pred[256,8192]{0,1:T(8,128)(4,1)S(1)} %compare_or_fusion), kind=kLoop, calls=%fused_computation.3 | loop fusion | flops 41942016 | bytes 35659776 | tf_op jit(solution)/shard_map/reduce_sum | solution.py:25
  184.7 105.1 %all-gather.7.cloned.1.call-done = bf16[8192,128]{0,1:T(8,128)(2,1)} async-done(((bf16[128,128]{0,1:T(8,128)(2,1)}), bf16[8192,128]{0,1:T(8,128)(2,1)}) %all-gather.7.cloned.1.call-update) | async-done | bytes 2097168 | tf_op jit(solution)/shard_map/all_gather | solution.py:57
  289.8 0.0 copy-start.1
  289.8 14.8 %fusion.18 = f32[4,256,128]{1,2,0:T(8,128)S(1)} fusion(f32[8192,256,4]{1,0,2:T(8,128)} %get-tuple-element.11, f32[4,256]{1,0:T(4,128)S(1)} %get-tuple-element.9, pred[256,8192]{0,1:T(8,128)(4,1)S(1)} %compare_or_fusion, bf16[8192,128]{0,1:T(8,128)(2,1)} %all-gather.7.cloned.1.call-done, f32[4,256]{1,0:T(4,128)S(1)} %get-tuple-element.6, ...), kind=kOutput, calls=%fused_computation.19 | convolution fusion | flops 2189688832 | bytes 38285312 | tf_op jit(solution)/shard_map/hgsn,nhd->hgsd/dot_general | solution.py:26
  304.6 0.0 copy-done.1
  304.6 0.3 fusion.23
  304.9 127.6 %all-gather.9.cloned.1.call-done = bf16[512,4096]{0,1:T(8,128)(2,1)} async-done(((bf16[512,64]{0,1:T(8,128)(2,1)}), bf16[512,4096]{0,1:T(8,128)(2,1)}) %all-gather.9.cloned.1.call-update) | async-done | bytes 4194320 | tf_op jit(solution)/shard_map/all_gather | solution.py:69
  432.6 4.8 %convolution_convert_fusion = bf16[256,4096]{1,0:T(8,128)(2,1)} fusion(bf16[256,512]{0,1:T(8,128)(2,1)S(1)} %bitcast.85, bf16[512,4096]{0,1:T(8,128)(2,1)} %all-gather.9.cloned.1.call-done), kind=kOutput, calls=%fused_computation.9 | convolution fusion | flops 1074790400 | bytes 6553600 | tf_op jit(solution)/shard_map/dot_general | solution.py:70
  437.4 0.0 reduce-scatter.2.cloned.1.call-update
  437.5 38.6 %reduce-scatter.2.cloned.1.call-done = bf16[256,512]{1,0:T(8,128)(2,1)} async-done(((bf16[256,4096]{1,0:T(8,128)(2,1)}), bf16[256,512]{1,0:T(8,128)(2,1)}) %reduce-scatter.2.cloned.1.call-update) | async-done | bytes 262160 | tf_op jit(solution)/shard_map/reduce_scatter | solution.py:71
  (5 shorter events, 0.0 us)
Async XLA Ops:
  6.5 90.4 %copy-start = (bf16[256,512]{1,0:T(8,128)(2,1)S(1)}, bf16[256,512]{1,0:T(8,128)(2,1)}, u32[]{:S(2)}) copy-start(bf16[256,512]{1,0:T(8,128)(2,1)} %param.8) | copy-start | bytes 786436
  6.5 148.0 %all-gather.5.cloned.1.call-start = ((), (), s32[]{:S(2)}) async-start(), calls=%async_computation.1 | async-start | bytes 2129920 | tf_op jit(solution)/shard_map/all_gather | solution.py:56
  7.3 282.5 %all-gather.7.cloned.1.call-start = ((), (), s32[]{:S(2)}) async-start(), calls=%async_computation.2 | async-start | bytes 2129920 | tf_op jit(solution)/shard_map/all_gather | solution.py:57
  8.8 423.8 %all-gather.9.cloned.1.call-start = ((), (), s32[]{:S(2)}) async-start(), calls=%async_computation.3 | async-start | bytes 4259840 | tf_op jit(solution)/shard_map/all_gather | solution.py:69
  9.5 466.5 %reduce-scatter.2.cloned.1.call-start = ((), (), s32[]{:S(2)}) async-start(), calls=%async_computation.4 | async-start | bytes 2359296 | tf_op jit(solution)/shard_map/reduce_scatter | solution.py:71
  289.8 14.8 %copy-start.1 = (bf16[256,128]{1,0:T(8,128)(2,1)S(1)}, bf16[256,128]{1,0:T(8,128)(2,1)}, u32[]{:S(2)}) copy-start(bf16[256,128]{1,0:T(8,128)(2,1)} %param.10) | copy-start | bytes 196612
Sparse Core Ops, SparseCore 0:
  10.3 144.2 all-gather.4
  157.4 132.2 all-gather.6
  292.7 139.8 all-gather.8
  437.6 38.4 reduce-scatter.1
where the time goes:
time: 483 us
  waiting for transfers between devices  329 us (68%)
  blocking collectives  78.8 us (16%)
  matrix products  36 us (7%)
  other arithmetic  23.1 us (5%)
  between operations  13.9 us (3%)
    all_gather x1, waiting for transfers between devices, local(): whole_weight = lax.all_gather(out_weight, 'seq', axis=1, tiled=True)  128 us
    all_gather x1, waiting for transfers between devices, local(): values = lax.all_gather(prefix_v, 'seq', axis=0, tiled=True)  105 us
    all_gather x1, blocking collectives, local(): positions = lax.all_gather(prefix_pos, 'seq', axis=0, tiled=True)  78.8 us
    all_gather x1, waiting for transfers between devices, local(): keys = lax.all_gather(prefix_k, 'seq', axis=0, tiled=True)  56.4 us
    reduce_scatter x1, waiting for transfers between devices, local(): lax.psum_scatter(partial_out.astype(jnp.bfloat16), 'tp', scatter_dimensio...  38.6 us
    dot_general x2, matrix products, update(): jnp.einsum('shgd,nhd->hgsn', grouped, key_heads, preferred_element_type=j...  16 us
    reduce_sum x2, other arithmetic, update(): run_sum = run_sum * factor + jnp.sum(weights, axis=-1)  15.2 us
    dot_general x2, matrix products, update(): jnp.einsum('hgsn,nhd->hgsd', weights.astype(jnp.bfloat16), value_heads, p...  15.1 us
  transfers between devices with their start and end apart: 4, of which 4 were waited for; matrix products, arithmetic and copies ran while one was open for 12% of the time, Pallas kernels for 0%

commit v1 on v0

v1 whole, which is shorter than its diff:
```python
import functools
import math

import jax
import jax.numpy as jnp
from jax import lax
from jax.experimental import pallas as pl
from jax.experimental.pallas import tpu as pltpu
from jax.sharding import PartitionSpec as P

HD = 128
SINKS = 4
NX = 4
MESH = pl.DeviceIdType.MESH
LOG2E = 1.4426950408889634


def gather_kernel(nz, a_ref, b_ref, i_ref, ga, gb, gi, sa, sb, si, ra_x, rb_z, ra_z, ri_x, ri_z, rb_x, own):
    half = nz // 2
    rows_b = b_ref.shape[0]
    low = rows_b // 2
    me = lax.axis_index("seq")
    x, z = me // nz, lax.rem(me, nz)
    count = NX * nz

    def slot(dx, dz):
        return lax.rem(x + dx + NX, NX) * nz + lax.rem(z + dz + nz, nz)

    def dev(dx, dz):
        return {"seq": slot(dx, dz)}

    right, left, up, down = dev(1, 0), dev(-1, 0), dev(0, 1), dev(0, -1)
    barrier = pltpu.get_barrier_semaphore()
    for peer in (right, left, dev(2, 0), up, down):
        pl.semaphore_signal(barrier, inc=1, device_id=peer, device_id_type=MESH)
    pl.semaphore_wait(barrier, 5)

    def push(src, dst, ssem, rsem, to):
        pltpu.make_async_remote_copy(
            src_ref=src, dst_ref=dst, send_sem=ssem, recv_sem=rsem, device_id=to, device_id_type=MESH
        ).start()

    def arrived(ref, sem):
        pltpu.make_async_copy(ref, ref, sem).wait()

    keep = [
        pltpu.make_async_copy(a_ref, ga.at[me], own.at[0]),
        pltpu.make_async_copy(b_ref, gb.at[me], own.at[1]),
        pltpu.make_async_copy(i_ref, gi.at[me], own.at[2]),
    ]

    def a_move(dx, dist, way):
        at = slot(dx, -way * dist)
        src = a_ref if (dx == 0 and dist == 0) else ga.at[at]
        sem = ra_z.at[dx, 0 if way > 0 else 1, dist]
        push(src, ga.at[at], sa, sem, up if way > 0 else down)

    def i_move(dx, dist, way):
        at = slot(dx, -way * dist)
        src = i_ref if (dx == 0 and dist == 0) else gi.at[at]
        sem = ri_z.at[dx, 0 if way > 0 else 1, dist]
        push(src, gi.at[at], si, sem, up if way > 0 else down)

    def b_move(dist, way):
        at = slot(0, -way * dist)
        src = b_ref if dist == 0 else gb.at[at]
        push(src, gb.at[at], sb, rb_z.at[0 if way > 0 else 1, dist], up if way > 0 else down)

    def b_side(dist, way):
        at = slot(0, -way * dist)
        src = b_ref if dist == 0 else gb.at[at]
        lane = 0 if way > 0 else 1
        push(src, gb.at[at], sb, rb_x.at[0, lane, dist], right)
        push(src, gb.at[at], sb, rb_x.at[1, lane, dist], left)

    def b_relay(dist, way):
        lane = 0 if way > 0 else 1
        at = slot(-1, -way * dist)
        arrived(gb.at[at], rb_x.at[0, lane, dist])
        push(gb.at[at, pl.ds(0, low)], gb.at[at, pl.ds(0, low)], sb, rb_x.at[2, lane, dist], right)
        at = slot(1, -way * dist)
        arrived(gb.at[at], rb_x.at[1, lane, dist])
        rest = pl.ds(low, rows_b - low)
        push(gb.at[at, rest], gb.at[at, rest], sb, rb_x.at[3, lane, dist], left)

    for dx in (1, 3, 2):
        push(a_ref, ga.at[me], sa, ra_x.at[dx], dev(dx, 0))
        push(i_ref, gi.at[me], si, ri_x.at[dx], dev(dx, 0))
    b_move(0, 1)
    b_move(0, -1)
    b_side(0, 1)
    a_move(0, 0, 1)
    a_move(0, 0, -1)
    i_move(0, 0, 1)
    i_move(0, 0, -1)
    for copy in keep:
        copy.start()
    for dx in (1, 3, 2):
        arrived(ga.at[slot(dx, 0)], ra_x.at[NX - dx])
        a_move(dx, 0, 1)
        a_move(dx, 0, -1)
        arrived(gi.at[slot(dx, 0)], ri_x.at[NX - dx])
        i_move(dx, 0, 1)
        i_move(dx, 0, -1)
    for k in range(1, half + 1):
        for way in (1, -1):
            last = half if way > 0 else half - 1
            lane = 0 if way > 0 else 1
            if k <= last:
                arrived(gb.at[slot(0, -way * k)], rb_z.at[lane, k - 1])
                if k < last:
                    b_move(k, way)
                b_side(k, way)
        for dx in (0, 1, 3, 2):
            for way in (1, -1):
                last = half if way > 0 else half - 1
                lane = 0 if way > 0 else 1
                if k <= last:
                    arrived(ga.at[slot(dx, -way * k)], ra_z.at[dx, lane, k - 1])
                    if k < last:
                        a_move(dx, k, way)
                    arrived(gi.at[slot(dx, -way * k)], ri_z.at[dx, lane, k - 1])
                    if k < last:
                        i_move(dx, k, way)
        for way in (1, -1):
            if k - 1 == 0 and way < 0:
                continue
            b_relay(k - 1, way)
    b_relay(half, 1)
    for dist in range(half + 1):
        for way in (1, -1):
            if way < 0 and (dist == 0 or dist == half):
                continue
            lane = 0 if way > 0 else 1
            at = slot(2, -way * dist)
            arrived(gb.at[at, pl.ds(0, low)], rb_x.at[2, lane, dist])
            arrived(gb.at[at, pl.ds(low, rows_b - low)], rb_x.at[3, lane, dist])
    for copy in keep:
        copy.wait()
    arrived(ga.at[pl.ds(0, count - 1)], sa)
    arrived(gb.at[pl.ds(0, count - 1)], sb)
    arrived(gi.at[pl.ds(0, count - 1)], si)


def gather(nz, pa, pb, ids):
    count = NX * nz
    half = nz // 2
    anywhere = pl.BlockSpec(memory_space=pl.ANY)
    dma = pltpu.SemaphoreType.DMA
    return pl.pallas_call(
        functools.partial(gather_kernel, nz),
        out_shape=(
            jax.ShapeDtypeStruct((count,) + pa.shape, pa.dtype),
            jax.ShapeDtypeStruct((count,) + pb.shape, pb.dtype),
            jax.ShapeDtypeStruct((count,) + ids.shape, ids.dtype),
        ),
        in_specs=[anywhere] * 3,
        out_specs=(anywhere,) * 3,
        scratch_shapes=[
            dma, dma, dma,
            dma((NX,)),
            dma((2, half)),
            dma((NX, 2, half)),
            dma((NX,)),
            dma((NX, 2, half)),
            dma((4, 2, half + 1)),
            dma((3,)),
        ],
        compiler_params=pltpu.CompilerParams(collective_id=0, has_side_effects=True),
        name="gather",
    )(pa, pb, ids)


def attend_kernel(q_ref, sk_ref, sv_ref, row_ref, col_ref, gi, ga, gb, out_ref,
                  ks, vs, scores, att, inv_v, inv_s, sem):
    count = ga.shape[0]
    first = count // 2
    tokens = q_ref.shape[0]
    heads = q_ref.shape[1] // HD
    main = first * HD
    total = main + HD + tokens
    tile = 512
    lane = lax.broadcasted_iota(jnp.int32, (1, HD), 1)
    which = lax.broadcasted_iota(jnp.int32, (count, 1, HD), 0)
    inv_v[...] = jnp.sum(jnp.where(gi[...] == lane[None], which, 0), axis=0)
    copy = pltpu.make_async_copy(inv_v, inv_s, sem)
    copy.start()
    copy.wait()

    def fill(i, _):
        at = inv_s[0, first + i]
        to = pl.multiple_of(i * HD, HD)
        ks[pl.ds(to, HD), :] = ga[at, :HD, :]
        vs[pl.ds(to, HD), :] = gb[at, :HD, :]
        return 0

    lax.fori_loop(0, first, fill, 0)
    at = inv_s[0, 0]
    ks[main:main + HD, :] = ga[at, :HD, :]
    vs[main:main + HD, :] = gb[at, :HD, :]
    ks[main + HD:, :] = sk_ref[...]
    vs[main + HD:, :] = sv_ref[...]

    same = col_ref[...] == row_ref[...]
    mine = lax.broadcasted_iota(jnp.int32, (tokens, tokens), 0)
    other = lax.broadcasted_iota(jnp.int32, (tokens, tokens), 1)
    offset = jnp.sum(jnp.where(same & (other < mine), 1.0, 0.0), axis=1, keepdims=True)
    lane_f = lane.astype(jnp.float32)
    edge = lane_f > offset
    own = same & (other <= mine)
    sink = lane < SINKS
    low = jnp.float32(-1e30)
    gain = jnp.float32(LOG2E / math.sqrt(HD))
    bounds = [(t, min(tile, total - t)) for t in range(0, main, tile)] + [(main, total - main)]

    def nt(a, b):
        return lax.dot_general(a, b, (((1,), (1,)), ((), ())), preferred_element_type=jnp.float32)

    for h in range(heads):
        q = q_ref[:, h * HD:(h + 1) * HD]
        top = jnp.full((tokens, HD), low, jnp.float32)
        for start, size in bounds:
            s = nt(q, ks[start:start + size, :])
            parts = [s[:, j:j + HD] for j in range(0, size, HD)]
            if start == 0:
                parts[0] = jnp.where(edge, parts[0], low)
            if start == main:
                parts[0] = jnp.where(sink, parts[0], low)
                for j in range(1, len(parts)):
                    parts[j] = jnp.where(own[:, (j - 1) * HD:j * HD], parts[j], low)
            for j, part in enumerate(parts):
                scores[:, start + j * HD:start + (j + 1) * HD] = part
                top = jnp.maximum(top, part)
        top = jnp.max(top, axis=1, keepdims=True)
        sums = jnp.zeros((tokens, HD), jnp.float32)
        acc = jnp.zeros((tokens, HD), jnp.float32)
        for start, size in bounds:
            w = jnp.exp2((scores[:, start:start + size] - top) * gain)
            for j in range(0, size, HD):
                sums = sums + w[:, j:j + HD]
            acc = acc + jnp.dot(w.astype(jnp.bfloat16), vs[start:start + size, :],
                                preferred_element_type=jnp.float32)
        att[:, h * HD:(h + 1) * HD] = (acc / jnp.sum(sums, axis=1, keepdims=True)).astype(jnp.bfloat16)

    cols = (ga.shape[1] - HD)
    group = tile // cols

    def project(g, _):
        pieces = []
        for h in range(heads):
            if h == 0:
                part = ga[pl.ds(g * group, group), HD:, :]
            else:
                part = gb[pl.ds(g * group, group), HD + (h - 1) * cols:HD + h * cols, :]
            pieces.append(part.reshape(group * cols, HD))
        w = jnp.concatenate(pieces, axis=1)
        to = pl.multiple_of(g * tile, tile)
        out_ref[:, pl.ds(to, tile)] = nt(att[...], w).astype(jnp.bfloat16)
        return 0

    lax.fori_loop(0, count // group, project, 0)


def attend(queries, suffix_k, suffix_v, row, col, gi, ga, gb):
    count = ga.shape[0]
    tokens = queries.shape[0]
    total = count // 2 * HD + HD + tokens
    width = count * (ga.shape[1] - HD)
    return pl.pallas_call(
        attend_kernel,
        out_shape=jax.ShapeDtypeStruct((tokens, width), jnp.bfloat16),
        scratch_shapes=[
            pltpu.VMEM((total, HD), jnp.bfloat16),
            pltpu.VMEM((total, HD), jnp.bfloat16),
            pltpu.VMEM((tokens, total), jnp.float32),
            pltpu.VMEM((tokens, queries.shape[1]), jnp.bfloat16),
            pltpu.VMEM((1, HD), jnp.int32),
            pltpu.SMEM((1, HD), jnp.int32),
            pltpu.SemaphoreType.DMA,
        ],
        compiler_params=pltpu.CompilerParams(vmem_limit_bytes=56 * 2**20),
        name="attend",
    )(queries, suffix_k, suffix_v, row, col, gi, ga, gb)


def local(queries, suffix_k, suffix_v, prefix_k, prefix_v, prefix_block, request_ids, out_weight):
    nz = lax.axis_size("seq") // NX
    cols = out_weight.shape[1]
    heads = out_weight.shape[0] // HD
    flipped = out_weight.T
    pieces = [flipped[:, h * HD:(h + 1) * HD] for h in range(heads)]
    pa = jnp.concatenate([prefix_k] + pieces[:1], axis=0)
    pb = jnp.concatenate([prefix_v] + pieces[1:], axis=0)
    ids = jnp.broadcast_to(prefix_block[:, None], (1, HD))
    ga, gb, gi = gather(nz, pa, pb, ids)
    col = request_ids.reshape(-1, 1)
    partial_out = attend(queries, suffix_k, suffix_v, request_ids, col, gi, ga, gb)
    return lax.psum_scatter(partial_out, "tp", scatter_dimension=1, tiled=True)


def solution(mesh):
    placed = (
        P("seq", "tp"),
        P("seq", "tp"),
        P("seq", "tp"),
        P("seq", "tp"),
        P("seq", "tp"),
        P("seq"),
        P("seq", None),
        P("tp", "seq"),
    )
    return jax.shard_map(
        local, mesh=mesh, in_specs=placed, out_specs=P("seq", "tp"), check_vma=False
    )
```

time: 483 us -> 143 us (0.30)
  waiting for transfers between devices: 329 us -> 37.1 us
  Pallas kernels: 0 us -> 85.9 us
  blocking collectives: 78.8 us -> 0 us
  matrix products: 36 us -> 0 us
  other arithmetic: 23.1 us -> 2.77 us
    all_gather x3 -> x0, waiting for transfers between devices: 289 us -> none  [the longest x1 128 us: local(): whole_weight = lax.all_gather(out_weight, 'seq', axis=1, tiled=True)]
    pallas_call x0 -> x2, Pallas kernels: none -> 85.9 us  [the longest x1 70.5 us: gather(): pl.pallas_call(functools.partial(gather_kernel, nz), out_shape=(jax.Shape...]
    all_gather x1 -> x0, blocking collectives: 78.8 us -> none  [local(): positions = lax.all_gather(prefix_pos, 'seq', axis=0, tiled=True)]
    dot_general x5 -> x0, matrix products: 36 us -> none  [the longest x2 16 us: update(): jnp.einsum('shgd,nhd->hgsn', grouped, key_heads, preferred_element_type=j...]
    reduce_sum x3 -> x0, other arithmetic: 16.1 us -> none  [the longest x2 15.2 us: update(): run_sum = run_sum * factor + jnp.sum(weights, axis=-1)]
    or x1 -> x0, other arithmetic: 6.11 us -> none  [local(): (positions[None, :] >= query_pos[:, None] - window + 1) | (positions[None...]
  transfers between devices with their start and end apart: 4 -> 1, of which waited for: 4 -> 1; matrix products, arithmetic and copies ran while one was open for 12% -> 0% of each run, Pallas kernels for 0% -> 0%
where the time goes in v1:
time: 143 us
  Pallas kernels  85.9 us (60%)
  waiting for transfers between devices  37.1 us (26%)
  between operations  14.1 us (10%)
  local copies, waits for them, and re-layouts  2.81 us (2%)
  other arithmetic  2.77 us (2%)
    pallas_call x1, Pallas kernels, gather(): pl.pallas_call(functools.partial(gather_kernel, nz), out_shape=(jax.Shape...  70.5 us
    reduce_scatter x1, waiting for transfers between devices, local(): return lax.psum_scatter(partial_out, 'tp', scatter_dimension=1, tiled=True)  37.1 us
    pallas_call x1, Pallas kernels, attend(): pl.pallas_call(attend_kernel, out_shape=jax.ShapeDtypeStruct((tokens, wid...  15.4 us
  transfers between devices with their start and end apart: 1, of which 1 were waited for; matrix products, arithmetic and copies ran while one was open for 0% of the time, Pallas kernels for 0%

profile of v1, /device:TPU:6, one launch (start us, length us, event | category | flops | bytes accessed | tf_op | source)
XLA Modules:
  0.0 142.7 jit_solution(12353719344140382915)
XLA Ops:
  6.5 0.0 reduce-scatter.2.cloned.1.call-start
  7.2 0.8 fusion
  8.0 1.5 %copy.9.col_ref = s32[256,1]{1,0:T(8,128)} copy(s32[256,1]{0,1:T(1,128)} %bitcast.5) | data formatting | bytes 2048 | tf_op jit(solution)/shard_map/reshape | solution.py:296
  9.4 1.4 pad_maximum_fusion.1.a_ref
  10.8 1.4 pad_maximum_fusion.b_ref
  12.2 0.6 broadcast_in_dim.9.i_ref
  12.8 70.5 %gather.1 = (bf16[64,192,128]{2,1,0:T(8,128)(2,1)}, bf16[64,320,128]{2,1,0:T(8,128)(2,1)}, s32[64,1,128]{2,1,0:T(1,128)}) custom-call(bf16[192,128]{1,0:T(8,128)(2,1)} %pad_maximum_fusion.1.a_ref, bf16[320,128]{1,0:T(8,128)(2,1)} %pad_maximum_fusion.b_ref, s32[1,128]{1,0:T(1,128)} %broadcast_in_dim.9.i_ref), custom_call_target="tpu_custom_call" | custom-call | tf_op jit(solution)/shard_map/gather/pallas_call | solution.py:150
  83.3 15.4 %attend.1 = bf16[256,4096]{1,0:T(8,128)(2,1)} custom-call(bf16[256,512]{1,0:T(8,128)(2,1)} %q_ref.1, bf16[256,128]{1,0:T(8,128)(2,1)} %sk_ref.1, bf16[256,128]{1,0:T(8,128)(2,1)} %sv_ref.1, s32[1,256]{1,0:T(1,128)} %row_ref.1, s32[256,1]{1,0:T(8,128)} %copy.9.col_ref, s32[64,1,128]{2,1,0:T(1,128)} %get-tuple-element.8.gi, ...), custom_call_target="tpu_custom_call" | custom-call | tf_op jit(solution)/shard_map/attend/pallas_call | solution.py:269
  98.7 0.0 reduce-scatter.2.cloned.1.call-update
  98.7 37.1 %reduce-scatter.2.cloned.1.call-done = bf16[256,512]{1,0:T(8,128)(2,1)} async-done(((bf16[256,4096]{1,0:T(8,128)(2,1)}), bf16[256,512]{1,0:T(8,128)(2,1)}) %reduce-scatter.2.cloned.1.call-update) | async-done | bytes 262160 | tf_op jit(solution)/shard_map/reduce_scatter | solution.py:298
Async XLA Ops:
  6.5 129.3 %reduce-scatter.2.cloned.1.call-start = ((), (), s32[]{:S(2)}) async-start(), calls=%async_computation.1 | async-start | bytes 2359296 | tf_op jit(solution)/shard_map/reduce_scatter | solution.py:298
Sparse Core Ops, SparseCore 0:
  98.8 36.9 reduce-scatter.1

commit v2 on v0

v2 whole, which is shorter than its diff:
```python
import functools
import math

import jax
import jax.numpy as jnp
from jax import lax
from jax.experimental import pallas as pl
from jax.experimental.pallas import tpu as pltpu
from jax.sharding import PartitionSpec as P

HD = 128
SINKS = 4
NX = 4
NY = 4
PART = 96
MESH = pl.DeviceIdType.MESH
LOG2E = 1.4426950408889634


def push(src, dst, ssem, rsem, to):
    pltpu.make_async_remote_copy(
        src_ref=src, dst_ref=dst, send_sem=ssem, recv_sem=rsem, device_id=to, device_id_type=MESH
    ).start()


def arrived(ref, sem):
    pltpu.make_async_copy(ref, ref, sem).wait()


def nt(a, b):
    return lax.dot_general(a, b, (((1,), (1,)), ((), ())), preferred_element_type=jnp.float32)


class Rings:
    def __init__(self, nz, x, z, ga, gb, sems, gi=None, isems=None):
        self.nz, self.x, self.z, self.half = nz, x, z, nz // 2
        self.ga, self.gb, self.gi = ga, gb, gi
        self.sa, self.sb, self.ra_x, self.rb_z, self.ra_z, self.rb_x = sems
        if gi is not None:
            self.si, self.ri_x, self.ri_z = isems
        self.rows_b = gb.shape[1]
        self.low = self.rows_b // 2
        self.right, self.left = self.dev(1, 0), self.dev(-1, 0)
        self.ends = {1: self.dev(0, 1), -1: self.dev(0, -1)}

    def slot(self, dx, dz):
        return lax.rem(self.x + dx + NX, NX) * self.nz + lax.rem(self.z + dz + self.nz, self.nz)

    def dev(self, dx, dz):
        return {"seq": self.slot(dx, dz)}

    def last(self, way):
        return self.half if way > 0 else self.half - 1

    def a_move(self, dx, dist, way):
        at = self.slot(dx, -way * dist)
        lane = 0 if way > 0 else 1
        push(self.ga.at[at], self.ga.at[at], self.sa, self.ra_z.at[dx, lane, dist], self.ends[way])
        if self.gi is not None:
            push(self.gi.at[at], self.gi.at[at], self.si, self.ri_z.at[dx, lane, dist], self.ends[way])

    def a_wait(self, dx, dist, way):
        at = self.slot(dx, -way * dist)
        lane = 0 if way > 0 else 1
        arrived(self.ga.at[at], self.ra_z.at[dx, lane, dist - 1])
        if self.gi is not None:
            arrived(self.gi.at[at], self.ri_z.at[dx, lane, dist - 1])

    def b_move(self, dist, way):
        at = self.slot(0, -way * dist)
        push(self.gb.at[at], self.gb.at[at], self.sb, self.rb_z.at[0 if way > 0 else 1, dist], self.ends[way])

    def b_side(self, dist, way):
        at = self.slot(0, -way * dist)
        lane = 0 if way > 0 else 1
        push(self.gb.at[at], self.gb.at[at], self.sb, self.rb_x.at[0, lane, dist], self.right)
        push(self.gb.at[at], self.gb.at[at], self.sb, self.rb_x.at[1, lane, dist], self.left)

    def halves(self, at):
        return self.gb.at[at, pl.ds(0, self.low)], self.gb.at[at, pl.ds(self.low, self.rows_b - self.low)]

    def b_relay(self, dist, way):
        lane = 0 if way > 0 else 1
        at = self.slot(-1, -way * dist)
        arrived(self.gb.at[at], self.rb_x.at[0, lane, dist])
        part = self.halves(at)[0]
        push(part, part, self.sb, self.rb_x.at[2, lane, dist], self.right)
        at = self.slot(1, -way * dist)
        arrived(self.gb.at[at], self.rb_x.at[1, lane, dist])
        part = self.halves(at)[1]
        push(part, part, self.sb, self.rb_x.at[3, lane, dist], self.left)

    def begin(self):
        me = self.slot(0, 0)
        for dx in (1, 3, 2):
            push(self.ga.at[me], self.ga.at[me], self.sa, self.ra_x.at[dx], self.dev(dx, 0))
            if self.gi is not None:
                push(self.gi.at[me], self.gi.at[me], self.si, self.ri_x.at[dx], self.dev(dx, 0))
        self.b_move(0, 1)
        self.b_move(0, -1)
        self.b_side(0, 1)
        self.a_move(0, 0, 1)
        self.a_move(0, 0, -1)

    def spread(self):
        for dx in (1, 3, 2):
            arrived(self.ga.at[self.slot(dx, 0)], self.ra_x.at[NX - dx])
            if self.gi is not None:
                arrived(self.gi.at[self.slot(dx, 0)], self.ri_x.at[NX - dx])
            self.a_move(dx, 0, 1)
            self.a_move(dx, 0, -1)

    def step(self, k):
        for way in (1, -1):
            if k <= self.last(way):
                arrived(self.gb.at[self.slot(0, -way * k)], self.rb_z.at[0 if way > 0 else 1, k - 1])
                if k < self.last(way):
                    self.b_move(k, way)
                self.b_side(k, way)
        for dx in (0, 1, 3, 2):
            for way in (1, -1):
                if k <= self.last(way):
                    self.a_wait(dx, k, way)
                    if k < self.last(way):
                        self.a_move(dx, k, way)
        for way in (1, -1):
            if k - 1 > 0 or way > 0:
                self.b_relay(k - 1, way)

    def finish(self):
        self.b_relay(self.half, 1)
        for dist in range(self.half + 1):
            for way in (1, -1):
                if way < 0 and (dist == 0 or dist == self.half):
                    continue
                lane = 0 if way > 0 else 1
                low, high = self.halves(self.slot(2, -way * dist))
                arrived(low, self.rb_x.at[2, lane, dist])
                arrived(high, self.rb_x.at[3, lane, dist])

    def drain(self):
        count = NX * self.nz
        arrived(self.ga.at[pl.ds(0, count - 1)], self.sa)
        arrived(self.gb.at[pl.ds(0, count - 1)], self.sb)
        if self.gi is not None:
            arrived(self.gi.at[pl.ds(0, count - 1)], self.si)


def kernel(nz, q_ref, sk_ref, sv_ref, pk_ref, pv_ref, block_ref, row_ref, w_ref, out_ref,
           ga, gb, gi, wa, wb, wt, ks, vs, scores, att, inv_v, inv_s, sem, *sems):
    ring_sems, id_sems, w_sems = sems[0:6], sems[6:9], sems[9:15]
    sp, rp, sg, rg_y, rg_c = sems[15:]
    half = nz // 2
    count = NX * nz
    first = count // 2
    tokens = q_ref.shape[0]
    heads = q_ref.shape[1] // HD
    cols = w_ref.shape[1]
    me, t = lax.axis_index("seq"), lax.axis_index("tp")
    x, z, y, c = me // nz, lax.rem(me, nz), t // 2, lax.rem(t, 2)

    other_half = z // half
    w_slot = lax.rem(y + 1, NX) * nz + lax.rem(half * other_half + 2 * lax.rem(z, half) + c - nz // 4 + nz, nz)
    w_to = {"seq": w_slot, "tp": 2 * x + other_half}
    v = lax.rem(z + nz // 4 - half * c + nz, nz)
    w_from = {"seq": y * nz + half * c + v // 2, "tp": 2 * lax.rem(x + NX - 1, NX) + lax.rem(v, 2)}
    partner = {"tp": 2 * y + 1 - c}

    def column(dy):
        return 2 * lax.rem(y + dy, NY) + c

    kv = Rings(nz, x, z, ga, gb, ring_sems, gi, id_sems)
    wr = Rings(nz, x, z, wa, wb, w_sems)

    barrier = pltpu.get_barrier_semaphore()
    peers = [kv.dev(1, 0), kv.dev(-1, 0), kv.dev(2, 0), kv.dev(0, 1), kv.dev(0, -1), w_to, w_from, partner]
    peers = peers + [{"tp": column(dy)} for dy in range(1, NY)]
    for peer in peers:
        pl.semaphore_signal(barrier, inc=1, device_id=peer, device_id_type=MESH)

    ga[me] = pk_ref[:PART, :]
    gb[me, :HD, :] = pv_ref[...]
    gb[me, HD:, :] = pk_ref[PART:, :]
    gi[me] = jnp.full((1, HD), block_ref[0], jnp.int32)
    flipped = w_ref[...].astype(jnp.float32).T.astype(jnp.bfloat16)
    for h in range(heads):
        wt[h * cols:(h + 1) * cols, :] = flipped[:, h * HD:(h + 1) * HD]

    row = jnp.broadcast_to(row_ref[...].astype(jnp.float32), (tokens, tokens))
    col = row.T
    mine = lax.broadcasted_iota(jnp.int32, (tokens, tokens), 0)
    other = lax.broadcasted_iota(jnp.int32, (tokens, tokens), 1)
    same = jnp.where(row == col, 1.0, 0.0)
    offset = jnp.sum(jnp.where(other < mine, same, 0.0), axis=1, keepdims=True)
    lane = lax.broadcasted_iota(jnp.int32, (1, HD), 1)
    low = jnp.float32(-1e30)
    main = first * HD
    total = main + HD + tokens
    ks[main + HD:, :] = sk_ref[...]
    vs[main + HD:, :] = sv_ref[...]

    pl.semaphore_wait(barrier, len(peers))
    kv.begin()
    push(wt.at[pl.ds(0, PART)], wa.at[w_slot], sp, rp.at[0], w_to)
    push(wt.at[pl.ds(PART, wt.shape[0] - PART)], wb.at[w_slot], sp, rp.at[1], w_to)
    kv.spread()
    for k in range(1, half + 1):
        kv.step(k)
        if k == max(half - 1, 1):
            arrived(wa.at[me], rp.at[0])
            arrived(wb.at[me], rp.at[1])
            wr.begin()
    kv.finish()
    wr.spread()

    which = lax.broadcasted_iota(jnp.int32, (count, 1, HD), 0)
    inv_v[...] = jnp.max(jnp.where(gi[...] == lane[None], which, 0), axis=0)
    copy = pltpu.make_async_copy(inv_v, inv_s, sem)
    copy.start()
    copy.wait()

    def fetch(to, at):
        ks[pl.ds(to, PART), :] = ga[at]
        ks[pl.ds(to + PART, HD - PART), :] = gb[at, HD:, :]
        vs[pl.ds(to, HD), :] = gb[at, :HD, :]

    def fill(i, _):
        fetch(pl.multiple_of(i * HD, HD), inv_s[0, first + i])
        return 0

    lax.fori_loop(0, first, fill, 0)
    fetch(main, inv_s[0, 0])

    edge = lane.astype(jnp.float32) > offset
    own = (same > 0.5) & (other <= mine)
    sink = lane < SINKS
    gain = jnp.float32(LOG2E / math.sqrt(HD))
    tile = 512
    bounds = [(s, min(tile, total - s)) for s in range(0, main, tile)] + [(main, total - main)]

    def ag_send(h):
        at = t * heads + h
        for dy in (1, 3, 2):
            push(att.at[at], att.at[at], sg, rg_y.at[dy, h], {"tp": column(dy)})
        push(att.at[at], att.at[at], sg, rg_c.at[0, h], partner)

    def ag_relay(h):
        for dy in (1, 3, 2):
            at = column(dy) * heads + h
            arrived(att.at[at], rg_y.at[NY - dy, h])
            push(att.at[at], att.at[at], sg, rg_c.at[dy, h], partner)

    ticks = iter(range(1, half + 1))

    def tick():
        k = next(ticks, None)
        if k is not None:
            wr.step(k)

    for h in range(heads):
        q = q_ref[:, h * HD:(h + 1) * HD]
        top = jnp.full((tokens, HD), low, jnp.float32)
        for start, size in bounds:
            s = nt(q, ks[start:start + size, :])
            parts = [s[:, j:j + HD] for j in range(0, size, HD)]
            if start == 0:
                parts[0] = jnp.where(edge, parts[0], low)
            if start == main:
                parts[0] = jnp.where(sink, parts[0], low)
                for j in range(1, len(parts)):
                    parts[j] = jnp.where(own[:, (j - 1) * HD:j * HD], parts[j], low)
            for j, part in enumerate(parts):
                scores[:, start + j * HD:start + (j + 1) * HD] = part
                top = jnp.maximum(top, part)
        top = jnp.max(top, axis=1, keepdims=True)
        tick()
        sums = jnp.zeros((tokens, HD), jnp.float32)
        acc = jnp.zeros((tokens, HD), jnp.float32)
        for start, size in bounds:
            w = jnp.exp2((scores[:, start:start + size] - top) * gain)
            for j in range(0, size, HD):
                sums = sums + w[:, j:j + HD]
            acc = acc + jnp.dot(w.astype(jnp.bfloat16), vs[start:start + size, :],
                                preferred_element_type=jnp.float32)
        att[t * heads + h] = (acc / jnp.sum(sums, axis=1, keepdims=True)).astype(jnp.bfloat16)
        tick()
        ag_send(h)
        if h > 0:
            ag_relay(h - 1)
    ag_relay(heads - 1)
    for k in ticks:
        wr.step(k)
    wr.finish()
    for dy in range(NY):
        for h in range(heads):
            at = (2 * lax.rem(y + dy, NY) + 1 - c) * heads + h
            arrived(att.at[at], rg_c.at[dy, h])

    cut = PART - cols
    result = jnp.zeros((tokens, out_ref.shape[1]), jnp.float32)
    for yy in range(NY):
        for cc in range(2):
            base = ((yy + 1) % NX) * nz
            spots = [base + lax.rem(half * c - nz // 4 + cc + 2 * u + nz, nz) for u in range(half)]
            a = [wa[s] for s in spots]
            b = [wb[s] for s in spots]
            rest = cols - cut
            weight = [
                [p[:cols] for p in a],
                [piece for p, r in zip(a, b) for piece in (p[cols:], r[:rest])],
                [r[rest:rest + cols] for r in b],
                [r[rest + cols:] for r in b],
            ]
            w = jnp.concatenate([jnp.concatenate(pieces, axis=0) for pieces in weight], axis=1)
            from_t = (2 * yy + cc) * heads
            a = jnp.concatenate([att[from_t + h] for h in range(heads)], axis=1)
            result = result + nt(a, w)
    out_ref[...] = result.astype(out_ref.dtype)

    kv.drain()
    wr.drain()
    arrived(wt, sp)
    arrived(att.at[pl.ds(0, (NY - 1) * heads + NY * heads)], sg)


def local(queries, suffix_k, suffix_v, prefix_k, prefix_v, prefix_block, request_ids, out_weight):
    count = lax.axis_size("seq")
    nz = count // NX
    half = nz // 2
    tp = lax.axis_size("tp")
    tokens, width = queries.shape
    heads = width // HD
    cols = out_weight.shape[1]
    total = count // 2 * HD + HD + tokens
    bf = jnp.bfloat16
    dma = pltpu.SemaphoreType.DMA
    ring = [dma, dma, dma((NX,)), dma((2, half)), dma((NX, 2, half)), dma((4, 2, half + 1))]
    whole = pl.BlockSpec(memory_space=pltpu.VMEM)
    return pl.pallas_call(
        functools.partial(kernel, nz),
        out_shape=jax.ShapeDtypeStruct((tokens, cols * count // tp), bf),
        in_specs=[whole] * 5 + [pl.BlockSpec(memory_space=pltpu.SMEM)] + [whole] * 2,
        out_specs=whole,
        scratch_shapes=[
            pltpu.VMEM((count, PART, HD), bf),
            pltpu.VMEM((count, 2 * HD - PART, HD), bf),
            pltpu.VMEM((count, 1, HD), jnp.int32),
            pltpu.VMEM((count, PART, HD), bf),
            pltpu.VMEM((count, heads * cols - PART, HD), bf),
            pltpu.VMEM((heads * cols, HD), bf),
            pltpu.VMEM((total, HD), bf),
            pltpu.VMEM((total, HD), bf),
            pltpu.VMEM((tokens, total), jnp.float32),
            pltpu.VMEM((tp * heads, tokens, HD), bf),
            pltpu.VMEM((1, HD), jnp.int32),
            pltpu.SMEM((1, HD), jnp.int32),
            dma,
        ] + ring + [dma, dma((NX,)), dma((NX, 2, half))] + ring
        + [dma, dma((2,)), dma, dma((NY, heads)), dma((NY, heads))],
        compiler_params=pltpu.CompilerParams(
            collective_id=0, has_side_effects=True, vmem_limit_bytes=56 * 2**20
        ),
        name="block",
    )(queries, suffix_k, suffix_v, prefix_k, prefix_v, prefix_block, request_ids, out_weight)


def solution(mesh):
    placed = (
        P("seq", "tp"),
        P("seq", "tp"),
        P("seq", "tp"),
        P("seq", "tp"),
        P("seq", "tp"),
        P("seq"),
        P("seq", None),
        P("tp", "seq"),
    )
    return jax.shard_map(
        local, mesh=mesh, in_specs=placed, out_specs=P("seq", "tp"), check_vma=False
    )
```

time: 483 us -> 100 us (0.21)
  waiting for transfers between devices: 329 us -> 0 us
  Pallas kernels: 0 us -> 95.4 us
  blocking collectives: 78.8 us -> 0 us
  matrix products: 36 us -> 0 us
  other arithmetic: 23.1 us -> 0 us
  between operations: 13.9 us -> 0.66 us
    all_gather x3 -> x0, waiting for transfers between devices: 289 us -> none  [the longest x1 128 us: local(): whole_weight = lax.all_gather(out_weight, 'seq', axis=1, tiled=True)]
    pallas_call x0 -> x1, Pallas kernels: none -> 95.4 us  [local(): pl.pallas_call(functools.partial(kernel, nz), out_shape=jax.ShapeDtypeStr...]
    all_gather x1 -> x0, blocking collectives: 78.8 us -> none  [local(): positions = lax.all_gather(prefix_pos, 'seq', axis=0, tiled=True)]
    reduce_scatter x1 -> x0, waiting for transfers between devices: 38.6 us -> none  [local(): lax.psum_scatter(partial_out.astype(jnp.bfloat16), 'tp', scatter_dimensio...]
    dot_general x5 -> x0, matrix products: 36 us -> none  [the longest x2 16 us: update(): jnp.einsum('shgd,nhd->hgsn', grouped, key_heads, preferred_element_type=j...]
    reduce_sum x3 -> x0, other arithmetic: 16.1 us -> none  [the longest x2 15.2 us: update(): run_sum = run_sum * factor + jnp.sum(weights, axis=-1)]
    or x1 -> x0, other arithmetic: 6.11 us -> none  [local(): (positions[None, :] >= query_pos[:, None] - window + 1) | (positions[None...]
  transfers between devices with their start and end apart: 4 -> 0, of which waited for: 4 -> 0; matrix products, arithmetic and copies ran while one was open for 12% -> 0% of each run, Pallas kernels for 0% -> 0%
where the time goes in v2:
time: 100 us; the launch traced here: 99.3 us
  Pallas kernels  95.4 us (95%)
  local copies, waits for them, and re-layouts  3.27 us (3%)
    pallas_call x1, Pallas kernels, local(): pl.pallas_call(functools.partial(kernel, nz), out_shape=jax.ShapeDtypeStr...  95.4 us
    unnamed x2, local copies, waits for them, and re-layouts  3.27 us

profile of v2, /device:TPU:6, one launch (start us, length us, event | category | flops | bytes accessed | tf_op | source)
XLA Modules:
  0.0 99.3 jit_solution(10577192431992125192)
XLA Ops:
  0.7 1.6 %copy.9.w_ref = bf16[512,64]{1,0:T(8,128)(2,1)} copy(bf16[512,64]{0,1:T(8,128)(2,1)} %param.15) | data formatting | bytes 131072 | tf_op args[7]
  2.3 95.4 %block.1 = bf16[256,512]{1,0:T(8,128)(2,1)} custom-call(bf16[256,512]{1,0:T(8,128)(2,1)} %q_ref.1, bf16[256,128]{1,0:T(8,128)(2,1)} %sk_ref.1, bf16[256,128]{1,0:T(8,128)(2,1)} %sv_ref.1, bf16[128,128]{1,0:T(8,128)(2,1)} %pk_ref.1, bf16[128,128]{1,0:T(8,128)(2,1)} %pv_ref.1, s32[1]{0:T(128)S(6)} %copy.11.block_ref, s32[1,256]{1,0:T(1,128)} %row_ref.1, ...), custom_call_target="tpu_custom_call" | custom-call | tf_op jit(solution)/shard_map/block/pallas_call | solution.py:339
  97.6 1.7 %copy.12 = bf16[256,512]{1,0:T(8,128)(2,1)} copy(bf16[256,512]{1,0:T(8,128)(2,1)} %block.1) | data formatting | bytes 524288

commit v3 on v2

--- a/solution.py
+++ b/solution.py
@@ -13,6 +13,7 @@
 NX = 4
 NY = 4
 PART = 96
+LEAD = 2
 MESH = pl.DeviceIdType.MESH
 LOG2E = 1.4426950408889634
 
@@ -155,7 +156,7 @@
     first = count // 2
     tokens = q_ref.shape[0]
     heads = q_ref.shape[1] // HD
-    cols = w_ref.shape[1]
+    cols = w_ref.shape[0]
     me, t = lax.axis_index("seq"), lax.axis_index("tp")
     x, z, y, c = me // nz, lax.rem(me, nz), t // 2, lax.rem(t, 2)
 
@@ -182,9 +183,8 @@
     gb[me, :HD, :] = pv_ref[...]
     gb[me, HD:, :] = pk_ref[PART:, :]
     gi[me] = jnp.full((1, HD), block_ref[0], jnp.int32)
-    flipped = w_ref[...].astype(jnp.float32).T.astype(jnp.bfloat16)
     for h in range(heads):
-        wt[h * cols:(h + 1) * cols, :] = flipped[:, h * HD:(h + 1) * HD]
+        wt[h * cols:(h + 1) * cols, :] = w_ref[:, h * HD:(h + 1) * HD]
 
     row = jnp.broadcast_to(row_ref[...].astype(jnp.float32), (tokens, tokens))
     col = row.T
@@ -204,14 +204,17 @@
     push(wt.at[pl.ds(0, PART)], wa.at[w_slot], sp, rp.at[0], w_to)
     push(wt.at[pl.ds(PART, wt.shape[0] - PART)], wb.at[w_slot], sp, rp.at[1], w_to)
     kv.spread()
+    ahead = max(half - LEAD, 1)
     for k in range(1, half + 1):
         kv.step(k)
-        if k == max(half - 1, 1):
+        if k == ahead:
             arrived(wa.at[me], rp.at[0])
             arrived(wb.at[me], rp.at[1])
             wr.begin()
+            wr.spread()
+        elif k > ahead:
+            wr.step(k - ahead)
     kv.finish()
-    wr.spread()
 
     which = lax.broadcasted_iota(jnp.int32, (count, 1, HD), 0)
     inv_v[...] = jnp.max(jnp.where(gi[...] == lane[None], which, 0), axis=0)
@@ -250,7 +253,7 @@
             arrived(att.at[at], rg_y.at[NY - dy, h])
             push(att.at[at], att.at[at], sg, rg_c.at[dy, h], partner)
 
-    ticks = iter(range(1, half + 1))
+    ticks = iter(range(half - ahead + 1, half + 1))
 
     def tick():
         k = next(ticks, None)
@@ -361,7 +364,7 @@
             collective_id=0, has_side_effects=True, vmem_limit_bytes=56 * 2**20
         ),
         name="block",
-    )(queries, suffix_k, suffix_v, prefix_k, prefix_v, prefix_block, request_ids, out_weight)
+    )(queries, suffix_k, suffix_v, prefix_k, prefix_v, prefix_block, request_ids, out_weight.T)
 
 
 def solution(mesh):

time: 100 us -> 97.9 us (0.979)
  local copies, waits for them, and re-layouts: 3.27 us -> 1.67 us
    unnamed x2 -> x1, local copies, waits for them, and re-layouts: 3.27 us -> 1.67 us
where the time goes in v3:
time: 97.9 us; the launch traced here: 97.7 us
  Pallas kernels  95.4 us (97%)
  local copies, waits for them, and re-layouts  1.67 us (2%)
    pallas_call x1, Pallas kernels, local(): pl.pallas_call(functools.partial(kernel, nz), out_shape=jax.ShapeDtypeStr...  95.4 us

profile of v3, /device:TPU:6, one launch (start us, length us, event | category | flops | bytes accessed | tf_op | source)
XLA Modules:
  0.0 97.7 jit_solution(12567685714445012167)
XLA Ops:
  0.7 95.4 %block.1 = bf16[256,512]{1,0:T(8,128)(2,1)} custom-call(bf16[256,512]{1,0:T(8,128)(2,1)} %q_ref.1, bf16[256,128]{1,0:T(8,128)(2,1)} %sk_ref.1, bf16[256,128]{1,0:T(8,128)(2,1)} %sv_ref.1, bf16[128,128]{1,0:T(8,128)(2,1)} %pk_ref.1, bf16[128,128]{1,0:T(8,128)(2,1)} %pv_ref.1, s32[1]{0:T(128)S(6)} %copy.10.block_ref, s32[1,256]{1,0:T(1,128)} %row_ref.1, ...), custom_call_target="tpu_custom_call" | custom-call | tf_op jit(solution)/shard_map/block/pallas_call | solution.py:342
  96.0 1.7 %copy.11 = bf16[256,512]{1,0:T(8,128)(2,1)} copy(bf16[256,512]{1,0:T(8,128)(2,1)} %block.1) | data formatting | bytes 524288
